TPU v7x, 256 devices: a whole 4x4x8 slice. The times are simulated.
256 devices in a mesh: gr: 8 (over y, core), gc: 32 (over x, z).
Axes of the slice: x: 4, y: 4, z: 8, core: 2. Of those that a mesh axis runs over, the one named last changes fastest.
Arguments:
- below_factor: bfloat16 [31, 8, 64, 2, 32, 128], P(None, 'gr', None, None, 'gc'), may hold values from -0.046875 to 0.046875
- panel_factor: bfloat16 [31, 8, 64, 512], P(None, 'gr', 'gc'), may hold values from -0.046875 to 0.046875
- prior_factor: bfloat16 [512, 2, 32, 128], P('gr', None, 'gc'), may hold values from -0.25 to 0.25
- diag_factor: float32 [512, 512], replicated, may hold values from -1 to 3, as said below
- diag_inverse: float32 [512, 512], replicated, may hold values from -2 to 1, as said below
- below_adjoint: bfloat16 [31, 8, 64, 2, 32, 128], P(None, 'gr', None, None, 'gc'), may hold values from -6 to 6
- panel_adjoint: bfloat16 [31, 8, 64, 512], P(None, 'gr', 'gc'), may hold values from -6 to 6
- prior_adjoint: bfloat16 [512, 2, 32, 128], P('gr', None, 'gc'), may hold values from -6 to 6
- diag_adjoint: float32 [512, 512], replicated, may hold values from -6 to 6
Outputs:
- below_update: bfloat16 [31, 8, 64, 2, 32, 128], P(None, 'gr', None, None, 'gc')
- panel_gradient: bfloat16 [31, 8, 64, 512], P(None, 'gr', 'gc')
- prior_update: bfloat16 [512, 2, 32, 128], P('gr', None, 'gc')
- diag_gradient: float32 [512, 512], replicated
Inputs may be any that keep to these rules, and one draw needn't show every extreme that they name: `diag_factor`: lower triangular, diagonal entries positive. `diag_inverse`: the inverse of diag_factor.
All inputs are finite; a program needn't handle non-finite values.
Results may differ from a plain program's by a relative error of at most 0.015.
Values may be sent and summed in bfloat16 or wider, within the bound.
A program may use at most 64 MiB of HBM per device.

v0:
```python
import jax
import jax.numpy as jnp
from jax import lax
from jax.sharding import PartitionSpec as P


def row_product(left_rows, right_rows):
    return lax.dot_general(
        left_rows, right_rows, (((0,), (0,)), ((), ())), preferred_element_type=jnp.float32
    )


def diag_solve(diag_factor, diag_inverse, diag_reduced):
    highest = lax.Precision.HIGHEST
    chol_proj = jnp.dot(diag_factor.T, diag_reduced, precision=highest)
    phi_lower = jnp.tril(chol_proj) - 0.5 * jnp.diag(jnp.diagonal(chol_proj))
    symmetric = 0.5 * (phi_lower + phi_lower.T)
    left_side = jnp.dot(diag_inverse.T, symmetric, precision=highest)
    return jnp.dot(left_side, diag_inverse, precision=highest)


def local(
    below_factor,
    panel_factor,
    prior_factor,
    diag_factor,
    diag_inverse,
    below_adjoint,
    panel_adjoint,
    prior_adjoint,
    diag_adjoint,
):
    tile_count = below_factor.shape[0]
    tile_rows = below_factor.shape[2]
    local_rows = tile_count * tile_rows
    local_cols = below_factor.shape[3] * below_factor.shape[5]
    own_rows = panel_factor.shape[2]
    width = panel_factor.shape[3]
    prior_local = prior_factor.shape[0]
    below_mat = below_factor.reshape(local_rows, local_cols)
    below_bar = below_adjoint.reshape(local_rows, local_cols)
    inverse_bf = diag_inverse.astype(jnp.bfloat16)
    whole_bar, whole_factor = (
        lax.all_gather(panel_adjoint, "gc", axis=2, tiled=True),
        lax.all_gather(panel_factor, "gc", axis=2, tiled=True),
    )
    grad_rows = jnp.dot(
        whole_bar.reshape(local_rows, width), inverse_bf, preferred_element_type=jnp.float32
    ).astype(jnp.bfloat16)
    summed = lax.psum(
        row_product(grad_rows, whole_factor.reshape(local_rows, width)).astype(jnp.bfloat16), "gr"
    ).astype(jnp.float32)
    grid_col = lax.axis_index("gc")
    panel_grad = lax.dynamic_slice_in_dim(
        grad_rows.reshape(tile_count, 1, tile_rows, width), grid_col * own_rows, own_rows, 2
    )
    diag_reduced = jnp.tril(diag_adjoint - summed)
    diag_gradient = diag_solve(diag_factor, diag_inverse, diag_reduced)
    prior_here = prior_factor.reshape(prior_local, local_cols)
    prior_whole = lax.all_gather(prior_here, "gr", axis=0, tiled=True)
    below_new = (
        below_bar.astype(jnp.float32)
        - jnp.dot(grad_rows, prior_whole, preferred_element_type=jnp.float32)
    ).astype(jnp.bfloat16)
    crossing = lax.psum_scatter(
        row_product(grad_rows, below_mat).astype(jnp.bfloat16),
        "gr",
        scatter_dimension=0,
        tiled=True,
    ).astype(jnp.float32)
    grid_row = lax.axis_index("gr")
    twice_rows = lax.dynamic_slice_in_dim(
        2.0 * diag_gradient, grid_row * prior_local, prior_local, 0
    ).astype(jnp.bfloat16)
    curvature = jnp.dot(twice_rows, prior_whole, preferred_element_type=jnp.float32)
    prior_bar = prior_adjoint.reshape(prior_local, local_cols).astype(jnp.float32)
    prior_new = (prior_bar - crossing - curvature).astype(jnp.bfloat16)
    return (
        below_new.reshape(below_adjoint.shape),
        panel_grad,
        prior_new.reshape(prior_adjoint.shape),
        diag_gradient,
    )


def solution(mesh):
    in_specs = (
        P(None, "gr", None, None, "gc", None),
        P(None, "gr", "gc", None),
        P("gr", None, "gc", None),
        P(),
        P(),
        P(None, "gr", None, None, "gc", None),
        P(None, "gr", "gc", None),
        P("gr", None, "gc", None),
        P(),
    )
    out_specs = (
        P(None, "gr", None, None, "gc", None),
        P(None, "gr", "gc", None),
        P("gr", None, "gc", None),
        P(),
    )
    return jax.shard_map(local, mesh=mesh, in_specs=in_specs, out_specs=out_specs, check_vma=False)
```

profile of v0, /device:TPU:2, one launch (start us, length us, event | category | flops | bytes accessed | tf_op | source)
XLA Modules:
  0.0 281.4 jit_solution(9528895017282973600)
XLA Ops:
  7.2 0.0 all-gather.3.cloned.1.call-start
  7.2 1.6 copy.27
  8.8 0.0 all-gather.3.cloned.1.call-update
  8.8 0.0 all-gather.5.cloned.1.call-start
  8.9 1.5 copy.30
  10.3 0.0 all-gather.5.cloned.1.call-update
  10.4 0.0 all-reduce.2.cloned.1.call-start
  10.4 0.8 copy.46
  11.2 0.8 convert.3
  12.0 3.2 %convert.2 = f32[248,8,2,128]{3,2,1,0:T(2,128)} convert(bf16[248,8,2,128]{3,2,1,0:T(2,128)(2,1)} %bitcast.55) | non-fusion elementwise | flops 507904 | bytes 3047424
  15.2 13.3 %all_gather.10 = bf16[512,256]{1,0:T(8,128)(2,1)S(1)} all-gather(bf16[64,256]{1,0:T(8,128)(2,1)S(1)} %bitcast.57), channel_id=1, replica_groups=mesh['gr'=8,'gc'=32] {'gr'}, dimensions={0}, use_global_device_ids=true | all-gather | bytes 294912 | tf_op jit(solution)/shard_map/all_gather | solution.py:60
  28.5 62.4 %all-gather.3.cloned.1.call-done = bf16[31,1,64,512]{3,0,1,2:T(8,128)(2,1)} async-done(((bf16[31,1,2,512]{3,0,1,2:T(8,128)(2,1)}), bf16[31,1,64,512]{3,0,1,2:T(8,128)(2,1)}) %all-gather.3.cloned.1.call-update) | async-done | bytes 2031632 | tf_op jit(solution)/shard_map/all_gather | solution.py:44
  90.9 2.8 %copy.28 = bf16[31,1,64,512]{3,2,0,1:T(8,128)(2,1)S(1)} copy(bf16[31,1,64,512]{3,0,1,2:T(8,128)(2,1)} %all-gather.3.cloned.1.call-done) | data formatting | bytes 4063232 | tf_op jit(solution)/shard_map/all_gather | solution.py:44
  93.8 1.2 convolution_convert_fusion
  95.0 74.2 %all-gather.5.cloned.1.call-done = bf16[31,1,64,512]{3,0,1,2:T(8,128)(2,1)} async-done(((bf16[31,1,2,512]{3,0,1,2:T(8,128)(2,1)}), bf16[31,1,64,512]{3,0,1,2:T(8,128)(2,1)}) %all-gather.5.cloned.1.call-update) | async-done | bytes 2031632 | tf_op jit(solution)/shard_map/all_gather | solution.py:45
  169.2 2.7 copy.31
  172.0 2.1 convolution_convert_fusion.1
  174.1 0.0 all-reduce.2.cloned.1.call-update
  174.1 0.2 reduce-scatter.2.cloned.1.call-start
  174.3 3.2 %fusion = bf16[1984,256]{1,0:T(8,128)(2,1)} fusion(bf16[1984,512]{1,0:T(8,128)(2,1)S(1)} %convolution_convert_fusion, bf16[512,256]{1,0:T(8,128)(2,1)S(1)} %all_gather.10, f32[248,8,2,128]{3,2,1,0:T(2,128)} %convert.2), kind=kOutput, calls=%fused_computation.3 | convolution fusion | flops 521109504 | bytes 5341184 | tf_op jit(solution)/shard_map/dot_general | solution.py:63
  177.5 3.0 %reshape.38 = bf16[31,1,64,2,1,128]{5,3,2,0,4,1:T(2,128)(2,1)} reshape(bf16[1984,256]{1,0:T(8,128)(2,1)} %fusion) | data formatting | bytes 2031616 | tf_op jit(solution)/shard_map/reshape | solution.py:79
  180.6 0.7 constant_dynamic-slice_fusion
  181.3 2.7 convolution_convert_fusion.2
  184.0 54.5 %all-reduce.2.cloned.1.call-done = bf16[512,512]{1,0:T(8,128)(2,1)} async-done(((bf16[512,512]{1,0:T(8,128)(2,1)}), bf16[512,512]{1,0:T(8,128)(2,1)}) %all-reduce.2.cloned.1.call-update) | async-done | bytes 524304 | tf_op jit(solution)/shard_map/psum | solution.py:50
  238.5 3.2 %fusion.13 = f32[512,512]{1,0:T(8,128)S(1)} fusion(f32[512,512]{1,0:T(8,128)S(1)} %copy-done, f32[512,512]{1,0:T(8,128)} %param.17, bf16[512,512]{1,0:T(8,128)(2,1)} %all-reduce.2.cloned.1.call-done), kind=kOutput, calls=%fused_computation.22 | convolution fusion | flops 1611661312 | bytes 3670016 | tf_op jit(solution)/shard_map/dot_general | solution.py:15
  241.7 0.3 copy.32
  242.1 4.5 %gather_fusion = f32[512]{0:T(512)S(1)} fusion(f32[512,512]{1,0:T(8,128)S(1)} %bitcast.51, s32[512]{0:T(512)S(1)} %bitcast.50), kind=kCustom, calls=%fused_computation | custom fusion | bytes 8192 | tf_op jit(solution)/shard_map/jit(diagonal)/cond/branch_0_fun/gather | solution.py:16
  246.6 3.4 %fusion.2 = f32[512,512]{1,0:T(8,128)S(1)} fusion(f32[512,512]{1,0:T(8,128)} %param.13, f32[512,512]{1,0:T(8,128)S(1)} %fusion.13, f32[512]{0:T(512)S(1)} %gather_fusion, f32[512,512]{0,1:T(8,128)S(1)} %copy.32), kind=kOutput, calls=%fused_computation.8 | convolution fusion | flops 1614282752 | bytes 4196352 | tf_op jit(solution)/shard_map/dot_general | solution.py:18
  250.0 1.9 fusion.34
  251.9 21.4 %reduce-scatter.2.cloned.1.call-done = bf16[64,256]{1,0:T(8,128)(2,1)} async-done(((bf16[512,256]{1,0:T(8,128)(2,1)}), bf16[64,256]{1,0:T(8,128)(2,1)}) %reduce-scatter.2.cloned.1.call-update) | async-done | bytes 32784 | tf_op jit(solution)/shard_map/reduce_scatter | solution.py:65
  273.3 0.9 fusion.1
  274.3 0.6 reshape.42
  (10 shorter events, 0.0 us)
Async XLA Ops:
  7.2 231.3 %copy-start = (f32[512,512]{1,0:T(8,128)S(1)}, f32[512,512]{1,0:T(8,128)}, u32[]{:S(2)}) copy-start(f32[512,512]{1,0:T(8,128)} %param.12) | copy-start | bytes 3145732
  7.2 83.7 %all-gather.3.cloned.1.call-start = ((), (), s32[]{:S(2)}) async-start(), calls=%async_computation.1 | async-start | bytes 2162688 | tf_op jit(solution)/shard_map/all_gather | solution.py:44
  8.8 160.4 %all-gather.5.cloned.1.call-start = ((), (), s32[]{:S(2)}) async-start(), calls=%async_computation.3 | async-start | bytes 2162688 | tf_op jit(solution)/shard_map/all_gather | solution.py:45
  10.4 228.1 %all-reduce.2.cloned.1.call-start = ((), (), s32[]{:S(2)}) async-start(), calls=%async_computation.4 | async-start | bytes 1048576 | tf_op jit(solution)/shard_map/psum | solution.py:50
  90.9 2.8 %copy-start.2 = (f32[512,512]{1,0:T(8,128)S(1)}, f32[512,512]{1,0:T(8,128)}, u32[]{:S(2)}) copy-start(f32[512,512]{1,0:T(8,128)} %param.13) | copy-start | bytes 3145732
  174.1 99.2 %reduce-scatter.2.cloned.1.call-start = ((), (), s32[]{:S(2)}) async-start(), calls=%async_computation.2 | async-start | bytes 294912 | tf_op jit(solution)/shard_map/reduce_scatter | solution.py:65
  246.6 3.4 %copy-start.3 = (f32[512,512]{1,0:T(8,128)S(1)}, f32[512,512]{1,0:T(8,128)}, u32[]{:S(2)}) copy-start(f32[512,512]{1,0:T(8,128)} %param.13) | copy-start | bytes 3145732
  251.9 23.0 %copy-start.1 = (f32[512,512]{1,0:T(8,128)}, f32[512,512]{1,0:T(8,128)S(1)}, u32[]{:S(2)}) copy-start(f32[512,512]{1,0:T(8,128)S(1)} %fusion.34) | copy-start | bytes 3145732
Sparse Core Ops, SparseCore 0:
  11.2 79.6 all-gather.2
  94.1 75.1 all-gather.4
  174.2 64.2 all-reduce.1
  241.0 32.2 reduce-scatter.1
where the time goes:
time: 282 us; the launch traced here: 281 us
  waiting for transfers between devices  213 us (76%)
  matrix products  18.7 us (7%)
  local copies, waits for them, and re-layouts  18.6 us (7%)
  between operations  13.9 us (5%)
  blocking collectives  13.3 us (5%)
  other arithmetic  3.99 us (1%)
    all_gather x1, waiting for transfers between devices, local(): lax.all_gather(panel_factor, 'gc', axis=2, tiled=True)  74.2 us
    all_gather x1, waiting for transfers between devices, local(): lax.all_gather(panel_adjoint, 'gc', axis=2, tiled=True)  62.4 us
    psum x1, waiting for transfers between devices, local(): lax.psum(row_product(grad_rows, whole_factor.reshape(local_rows, width))....  54.5 us
    reduce_scatter x1, waiting for transfers between devices, local(): lax.psum_scatter(row_product(grad_rows, below_mat).astype(jnp.bfloat16),...  21.4 us
    all_gather x1, blocking collectives, local(): prior_whole = lax.all_gather(prior_here, 'gr', axis=0, tiled=True)  13.3 us
  transfers between devices with their start and end apart: 4, of which 4 were waited for; matrix products, arithmetic and copies ran while one was open for 12% of the time, Pallas kernels for 0%

commit v1 on v0

--- a/solution.py
+++ b/solution.py
@@ -2,6 +2,12 @@
 import jax.numpy as jnp
 from jax import lax
 from jax.sharding import PartitionSpec as P
+
+
+def gather_and_add(x, axis):
+    parts = lax.all_gather(x, axis, axis=0, tiled=False)
+    summed = parts.sum(axis=0)
+    return summed
 
 
 def row_product(left_rows, right_rows):
@@ -47,7 +53,7 @@
     grad_rows = jnp.dot(
         whole_bar.reshape(local_rows, width), inverse_bf, preferred_element_type=jnp.float32
     ).astype(jnp.bfloat16)
-    summed = lax.psum(
+    summed = gather_and_add(
         row_product(grad_rows, whole_factor.reshape(local_rows, width)).astype(jnp.bfloat16), "gr"
     ).astype(jnp.float32)
     grid_col = lax.axis_index("gc")

time: 282 us -> 251 us (0.89)
  waiting for transfers between devices: 213 us -> 178 us
    psum x1 -> x0, waiting for transfers between devices: 54.5 us -> none  [local(): lax.psum(row_product(grad_rows, whole_factor.reshape(local_rows, width))....]
    all_gather x1, waiting for transfers between devices: 62.4 us -> 80.5 us  [local(): lax.all_gather(panel_adjoint, 'gc', axis=2, tiled=True)]
    all_gather x0 -> x1, waiting for transfers between devices: none -> 6.93 us  [gather_and_add(): parts = lax.all_gather(x, axis, axis=0, tiled=False)]
    reduce_scatter x1, waiting for transfers between devices: 21.4 us -> 17.5 us  [local(): lax.psum_scatter(row_product(grad_rows, below_mat).astype(jnp.bfloat16),...]
    reduce_sum x0 -> x1, other arithmetic: none -> 3.14 us  [gather_and_add(): summed = parts.sum(axis=0)]
  transfers between devices with their start and end apart: 4 -> 4, of which waited for: 4 -> 4; matrix products, arithmetic and copies ran while one was open for 12% -> 15% of each run, Pallas kernels for 0% -> 0%
where the time goes in v1:
time: 251 us
  waiting for transfers between devices  178 us (71%)
  matrix products  19.9 us (8%)
  local copies, waits for them, and re-layouts  19 us (8%)
  between operations  13.9 us (6%)
  blocking collectives  13.4 us (5%)
  other arithmetic  6.39 us (3%)
    all_gather x1, waiting for transfers between devices, local(): lax.all_gather(panel_adjoint, 'gc', axis=2, tiled=True)  80.5 us
    all_gather x1, waiting for transfers between devices, local(): lax.all_gather(panel_factor, 'gc', axis=2, tiled=True)  73.1 us
    reduce_scatter x1, waiting for transfers between devices, local(): lax.psum_scatter(row_product(grad_rows, below_mat).astype(jnp.bfloat16),...  17.5 us
    all_gather x1, blocking collectives, local(): prior_whole = lax.all_gather(prior_here, 'gr', axis=0, tiled=True)  13.4 us
    all_gather x1, waiting for transfers between devices, gather_and_add(): parts = lax.all_gather(x, axis, axis=0, tiled=False)  6.93 us
  transfers between devices with their start and end apart: 4, of which 4 were waited for; matrix products, arithmetic and copies ran while one was open for 15% of the time, Pallas kernels for 0%

profile of v1, /device:TPU:2, one launch (start us, length us, event | category | flops | bytes accessed | tf_op | source)
XLA Modules:
  0.0 250.9 jit_solution(7678820566448938203)
XLA Ops:
  7.2 0.0 all-gather.5.cloned.1.call-start
  7.2 1.6 copy.27
  8.8 0.0 all-gather.5.cloned.1.call-update
  8.8 0.0 all-gather.7.cloned.1.call-start
  8.9 1.5 copy.30
  10.3 0.0 all-gather.7.cloned.1.call-update
  10.4 0.0 all-gather.9.cloned.1.call-start
  10.4 80.5 %all-gather.5.cloned.1.call-done = bf16[31,1,64,512]{3,0,1,2:T(8,128)(2,1)} async-done(((bf16[31,1,2,512]{3,0,1,2:T(8,128)(2,1)}), bf16[31,1,64,512]{3,0,1,2:T(8,128)(2,1)}) %all-gather.5.cloned.1.call-update) | async-done | bytes 2031632 | tf_op jit(solution)/shard_map/all_gather | solution.py:50
  90.9 2.7 %copy.28 = bf16[31,1,64,512]{3,2,0,1:T(8,128)(2,1)S(1)} copy(bf16[31,1,64,512]{3,0,1,2:T(8,128)(2,1)} %all-gather.5.cloned.1.call-done) | data formatting | bytes 4063232 | tf_op jit(solution)/shard_map/all_gather | solution.py:50
  93.7 2.4 convolution_convert_fusion
  96.1 73.1 %all-gather.7.cloned.1.call-done = bf16[31,1,64,512]{3,0,1,2:T(8,128)(2,1)} async-done(((bf16[31,1,2,512]{3,0,1,2:T(8,128)(2,1)}), bf16[31,1,64,512]{3,0,1,2:T(8,128)(2,1)}) %all-gather.7.cloned.1.call-update) | async-done | bytes 2031632 | tf_op jit(solution)/shard_map/all_gather | solution.py:51
  169.2 2.7 %copy.31 = bf16[31,1,64,512]{3,2,0,1:T(8,128)(2,1)S(1)} copy(bf16[31,1,64,512]{3,0,1,2:T(8,128)(2,1)} %all-gather.7.cloned.1.call-done) | data formatting | bytes 4063232 | tf_op jit(solution)/shard_map/all_gather | solution.py:51
  172.0 2.1 convolution_convert_fusion.1
  174.1 0.0 all-gather.9.cloned.1.call-update
  174.1 0.0 reduce-scatter.2.cloned.1.call-start
  174.2 3.2 %convert.3 = f32[248,8,2,128]{3,2,1,0:T(2,128)} convert(bf16[248,8,2,128]{3,2,1,0:T(2,128)(2,1)} %bitcast.57) | non-fusion elementwise | flops 507904 | bytes 3047424
  177.5 13.4 %all_gather.16 = bf16[512,256]{1,0:T(8,128)(2,1)S(1)} all-gather(bf16[64,256]{1,0:T(8,128)(2,1)S(1)} %bitcast.59), channel_id=1, replica_groups=mesh['gr'=8,'gc'=32] {'gr'}, dimensions={0}, use_global_device_ids=true | all-gather | bytes 294912 | tf_op jit(solution)/shard_map/all_gather | solution.py:66
  190.8 3.3 %fusion = bf16[1984,256]{1,0:T(8,128)(2,1)} fusion(bf16[1984,512]{1,0:T(8,128)(2,1)S(1)} %convolution_convert_fusion, bf16[512,256]{1,0:T(8,128)(2,1)S(1)} %all_gather.16, f32[248,8,2,128]{3,2,1,0:T(2,128)} %convert.3), kind=kOutput, calls=%fused_computation.3 | convolution fusion | flops 521109504 | bytes 5341184 | tf_op jit(solution)/shard_map/dot_general | solution.py:69
  194.1 3.1 %reshape.38 = bf16[31,1,64,2,1,128]{5,3,2,0,4,1:T(2,128)(2,1)} reshape(bf16[1984,256]{1,0:T(8,128)(2,1)} %fusion) | data formatting | bytes 2031616 | tf_op jit(solution)/shard_map/reshape | solution.py:85
  197.2 2.7 %convolution_convert_fusion.2 = bf16[512,256]{1,0:T(8,128)(2,1)} fusion(bf16[1984,512]{1,0:T(8,128)(2,1)S(1)} %convolution_convert_fusion, bf16[248,8,2,128]{3,2,1,0:T(2,128)(2,1)} %bitcast.63), kind=kOutput, calls=%fused_computation.5 | convolution fusion | flops 520224768 | bytes 3309568 | tf_op jit(solution)/shard_map/dot_general | solution.py:14
  199.8 0.0 reduce-scatter.2.cloned.1.call-update
  199.9 0.7 constant_dynamic-slice_fusion
  200.6 6.9 %all-gather.9.cloned.1.call-done = bf16[4096,512]{1,0:T(8,128)(2,1)} async-done(((bf16[512,512]{1,0:T(8,128)(2,1)}), bf16[4096,512]{1,0:T(8,128)(2,1)}) %all-gather.9.cloned.1.call-update) | async-done | bytes 4194320 | tf_op jit(solution)/shard_map/all_gather | solution.py:8
  207.5 3.1 %reduce_sum.12 = bf16[512,512]{1,0:T(8,128)(2,1)S(1)} reduce(bf16[8,512,512]{2,1,0:T(8,128)(2,1)} %bitcast.55, bf16[]{:T(256)} %constant.28.clone.1), dimensions={0}, to_apply=%region_1.2 | reduce | flops 1835008 | bytes 4718594 | tf_op jit(solution)/shard_map/reduce_sum | solution.py:9
  210.7 2.9 %fusion.13 = f32[512,512]{1,0:T(8,128)} fusion(f32[512,512]{1,0:T(8,128)S(1)} %copy-done, f32[512,512]{1,0:T(8,128)S(1)} %copy-done.2, bf16[512,512]{1,0:T(8,128)(2,1)S(1)} %reduce_sum.12), kind=kOutput, calls=%fused_computation.22 | convolution fusion | flops 1611661312 | bytes 3670016 | tf_op jit(solution)/shard_map/dot_general | solution.py:21
  213.5 1.6 copy.32
  215.1 4.5 %gather_fusion = f32[512]{0:T(512)S(1)} fusion(f32[512,512]{1,0:T(8,128)S(1)} %bitcast.52, s32[512]{0:T(512)S(1)} %bitcast.51), kind=kCustom, calls=%fused_computation | custom fusion | bytes 8192 | tf_op jit(solution)/shard_map/jit(diagonal)/cond/branch_0_fun/gather | solution.py:22
  219.6 3.7 %fusion.2 = f32[512,512]{1,0:T(8,128)S(1)} fusion(f32[512,512]{1,0:T(8,128)} %param.13, f32[512,512]{1,0:T(8,128)} %fusion.13, f32[512]{0:T(512)S(1)} %gather_fusion, f32[512,512]{0,1:T(8,128)S(1)} %copy.32), kind=kOutput, calls=%fused_computation.8 | convolution fusion | flops 1614282752 | bytes 4196352 | tf_op jit(solution)/shard_map/dot_general | solution.py:24
  223.3 1.9 fusion.34
  225.3 17.5 %reduce-scatter.2.cloned.1.call-done = bf16[64,256]{1,0:T(8,128)(2,1)} async-done(((bf16[512,256]{1,0:T(8,128)(2,1)}), bf16[64,256]{1,0:T(8,128)(2,1)}) %reduce-scatter.2.cloned.1.call-update) | async-done | bytes 32784 | tf_op jit(solution)/shard_map/reduce_scatter | solution.py:71
  242.8 0.9 fusion.1
  243.7 0.6 reshape.42
  (15 shorter events, 0.1 us)
Async XLA Ops:
  7.2 203.5 %copy-start = (f32[512,512]{1,0:T(8,128)S(1)}, f32[512,512]{1,0:T(8,128)}, u32[]{:S(2)}) copy-start(f32[512,512]{1,0:T(8,128)} %param.12) | copy-start | bytes 3145732
  7.2 83.7 %all-gather.5.cloned.1.call-start = ((), (), s32[]{:S(2)}) async-start(), calls=%async_computation.1 | async-start | bytes 2162688 | tf_op jit(solution)/shard_map/all_gather | solution.py:50
  8.8 160.4 %all-gather.7.cloned.1.call-start = ((), (), s32[]{:S(2)}) async-start(), calls=%async_computation.3 | async-start | bytes 2162688 | tf_op jit(solution)/shard_map/all_gather | solution.py:51
  10.4 197.1 %all-gather.9.cloned.1.call-start = ((), (), s32[]{:S(2)}) async-start(), calls=%async_computation.4 | async-start | bytes 4718592 | tf_op jit(solution)/shard_map/all_gather | solution.py:8
  172.0 2.2 copy-start.5
  172.0 2.2 copy-start.4
  174.1 68.6 %reduce-scatter.2.cloned.1.call-start = ((), (), s32[]{:S(2)}) async-start(), calls=%async_computation.2 | async-start | bytes 294912 | tf_op jit(solution)/shard_map/reduce_scatter | solution.py:71
  207.5 3.2 %copy-start.2 = (f32[512,512]{1,0:T(8,128)S(1)}, f32[512,512]{1,0:T(8,128)}, u32[]{:S(2)}) copy-start(f32[512,512]{1,0:T(8,128)} %param.17) | copy-start | bytes 3145732
  219.6 3.7 %copy-start.3 = (f32[512,512]{1,0:T(8,128)S(1)}, f32[512,512]{1,0:T(8,128)}, u32[]{:S(2)}) copy-start(f32[512,512]{1,0:T(8,128)} %param.13) | copy-start | bytes 3145732
  225.2 19.1 %copy-start.1 = (f32[512,512]{1,0:T(8,128)}, f32[512,512]{1,0:T(8,128)S(1)}, u32[]{:S(2)}) copy-start(f32[512,512]{1,0:T(8,128)S(1)} %fusion.34) | copy-start | bytes 3145732
Sparse Core Ops, SparseCore 0:
  11.2 79.6 all-gather.4
  94.1 75.1 all-gather.6
  174.2 33.2 all-gather.8
  209.9 32.8 reduce-scatter.1
